TPU v7x, 256 devices: a whole 4x4x8 slice. The times are simulated.
256 devices in a mesh: row: 16 (over z, y_lo), col: 16 (over y_hi, x, core).
Axes of the slice: x: 4, y: 4 (y_hi: 2, y_lo: 2; y = y_hi * 2 + y_lo), z: 8, core: 2. Of those that a mesh axis runs over, the one named last changes fastest.
Arguments:
- adjoint_source: float32 [192, 256, 2, 128], P('row', 'col'), may hold values from -6 to 6
- saved_currents: float32 [192, 256, 2, 128], P('row', 'col'), may hold values from -6 to 6
- lag_blocks: float32 [7, 7, 2, 128, 128], replicated, may hold values from -0.01875 to 0.01875
- element_inverse: float32 [2, 128, 128], replicated, may hold values from -0.088388348 to 1.0883883
Outputs:
- adjoint: float32 [192, 256, 2, 128], P('row', 'col')
- lag_grad: float32 [7, 7, 2, 128, 128], P(None, None, None, 'row')
All inputs are finite; a program needn't handle non-finite values.
Results may differ from a plain program's by a relative error of at most 0.0001.
Values sent between devices are 32-bit elements; how exact they have to be, the bound alone decides.
A program may use at most 128 MiB of HBM per device.

v0:
```python
import functools
import math

import jax
import jax.numpy as jnp
from jax import lax
from jax.experimental import pallas as pl
from jax.experimental.pallas import tpu as pltpu
from jax.sharding import PartitionSpec as P

SWEEPS = 2
F32 = jnp.float32
BF16 = jnp.bfloat16
MESH = pl.DeviceIdType.MESH
DIRS = tuple((dr, dc) for dr in (-1, 0, 1) for dc in (-1, 0, 1) if (dr, dc) != (0, 0))


def split(x):
    hi = x.astype(BF16)
    lo = (x - hi.astype(F32)).astype(BF16)
    return hi, lo


def dot(x, y):
    return jnp.dot(x, y, preferred_element_type=F32)


def put_embedded(dst, base, a0, a1):
    dst[pl.ds(base, 128), 0:128] = a0
    dst[pl.ds(base, 128), 128:256] = -a1
    dst[pl.ds(base + 128, 128), 0:128] = a1
    dst[pl.ds(base + 128, 128), 128:256] = a0


def field(ref, rows, start, cols):
    re = ref[rows, pl.ds(start, cols, stride=2), :]
    im = ref[rows, pl.ds(start + 1, cols, stride=2), :]
    return re, im


def sweeps_kernel(
    src, lag, inv, out,
    stage, whi, wlo, vhi, vlo, ext, shifted, acc, adj,
    lag_sem, send_sem, recv_sem,
):
    peers_r, peers_c = lax.axis_size("row"), lax.axis_size("col")
    r, c = lax.axis_index("row"), lax.axis_index("col")

    def lag_copy(a):
        return pltpu.make_async_copy(lag.at[a], stage.at[a], lag_sem.at[a])

    for a in range(7):
        lag_copy(a).start()

    def at(dr, dc):
        return (lax.rem(r + dr + peers_r, peers_r), lax.rem(c + dc + peers_c, peers_c))

    barrier = pltpu.get_barrier_semaphore()
    for dr, dc in DIRS:
        pl.semaphore_signal(barrier, inc=1, device_id=at(dr, dc), device_id_type=MESH)

    def box(dr, dc):
        rows = {-1: (3, 15, 3), 1: (12, 0, 3), 0: (3, 3, 12)}[dr]
        cols = {-1: (8, 40, 8), 1: (32, 0, 8), 0: (8, 8, 32)}[dc]
        return rows, cols

    def halo_copy(s, d):
        dr, dc = DIRS[d]
        (rs, rd, rn), (cs, cd, cn) = box(dr, dc)
        return pltpu.make_async_remote_copy(
            src_ref=ext.at[s, pl.ds(rs, rn), pl.ds(cs, cn), :],
            dst_ref=ext.at[s, pl.ds(rd, rn), pl.ds(cd, cn), :],
            send_sem=send_sem.at[s, d],
            recv_sem=recv_sem.at[s, d],
            device_id=at(dr, dc),
            device_id_type=MESH,
        )

    b0h, b0l = split(inv[0])
    b1h, b1l = split(inv[1])
    put_embedded(vhi, 0, b0h, b1h)
    put_embedded(vlo, 0, b0l, b1l)

    def apply_inverse(x):
        xh, xl = split(x)
        return dot(xh, vhi[...]) + dot(xl, vhi[...]) + dot(xh, vlo[...])

    def source():
        re, im = field(src, slice(None), 0, 16)
        return jnp.concatenate([re.reshape(192, 128), im.reshape(192, 128)], axis=1)

    def publish(ref, at_, x):
        rows, start = at_
        ref[rows, pl.ds(start, 16, stride=2), :] = x[:, :128].reshape(12, 16, 128)
        ref[rows, pl.ds(start + 1, 16, stride=2), :] = x[:, 128:].reshape(12, 16, 128)

    adj[...] = apply_inverse(source())
    publish(ext.at[0], (slice(3, 15), 8), adj[...])
    pl.semaphore_wait(barrier, len(DIRS))

    for s in range(SWEEPS):
        for d in range(len(DIRS)):
            halo_copy(s, d).start()
        if s == 0:
            def prepare(a, carry):
                lag_copy(a).wait()

                def one(b, carry):
                    h0, l0 = split(stage[a, b, 0])
                    h1, l1 = split(stage[a, b, 1])
                    base = pl.multiple_of(b * 256, 256)
                    put_embedded(whi.at[a], base, h0, h1)
                    put_embedded(wlo.at[a], base, l0, l1)
                    return carry

                return lax.fori_loop(0, 7, one, carry)

            lax.fori_loop(0, 7, prepare, 0)
        for d in range(len(DIRS)):
            halo_copy(s, d).wait_send()
        for d in range(len(DIRS)):
            halo_copy(s, d).wait_recv()

        @pl.when(r == 0)
        def _():
            ext[s, 0:3] = jnp.zeros((3, 48, 128), F32)

        @pl.when(r == peers_r - 1)
        def _():
            ext[s, 15:18] = jnp.zeros((3, 48, 128), F32)

        @pl.when(c == 0)
        def _():
            ext[s, :, 0:8, :] = jnp.zeros((18, 8, 128), F32)

        @pl.when(c == peers_c - 1)
        def _():
            ext[s, :, 40:48, :] = jnp.zeros((18, 8, 128), F32)

        for b in range(7):
            for h in range(2):
                hi, lo = split(ext[s, :, pl.ds(2 * (b + 1) + h, 16, stride=2), :])
                lanes = slice(b * 256 + h * 128, b * 256 + h * 128 + 128)
                shifted[:, 0:16, lanes] = hi
                shifted[:, 16:32, lanes] = lo

        acc[...] = jnp.zeros_like(acc)

        def lag_row(a, carry):
            both = dot(shifted[pl.ds(a, 12)].reshape(384, 1792), whi[a]).reshape(12, 32, 256)
            rest = dot(shifted[pl.ds(a, 12), 0:16, :].reshape(192, 1792), wlo[a])
            acc[...] += (both[:, 0:16] + both[:, 16:32]).reshape(192, 256) + rest
            return carry

        lax.fori_loop(0, 7, lag_row, 0)
        adj[...] += apply_inverse(source() - adj[...] - acc[...])
        if s + 1 < SWEEPS:
            publish(ext.at[s + 1], (slice(3, 15), 8), adj[...])
        else:
            publish(out, (slice(None), 0), adj[...])


def grads_kernel(
    factor, adj, cur, out,
    cg, chi, clo, at, ra, strip, a7h, a7l, acc, terms, gathered, piece, swapped, result,
    cg_send, cg_recv, ra_send, ra_recv, halo_send, halo_recv,
    red_send, red_recv, swap_send, swap_recv, res_send, res_recv, own_sem,
):
    n = 16
    r, c = lax.axis_index("row"), lax.axis_index("col")

    def wrap(x):
        return lax.rem(x + n, n)

    barrier = pltpu.get_barrier_semaphore()

    def greet(k, carry):
        pl.semaphore_signal(barrier, inc=1, device_id=(r, wrap(c + k)), device_id_type=MESH)
        pl.semaphore_signal(barrier, inc=1, device_id=(wrap(r + k), c), device_id_type=MESH)
        return carry

    lax.fori_loop(1, n, greet, 0)

    @pl.when(r != c)
    def _():
        pl.semaphore_signal(barrier, inc=1, device_id=(c, r), device_id_type=MESH)

    for h in range(2):
        part = adj[:, pl.ds(h, 16, stride=2), :].reshape(192, 128)
        part = jnp.concatenate([part, jnp.zeros((64, 128), F32)], axis=0)
        at[h] = part.T.reshape(16, 8, 256)

    own_current = pltpu.make_async_copy(cur, cg.at[c], own_sem.at[0])
    own_current.start()
    own_slice = pltpu.make_async_copy(at.at[:, c], ra.at[c], own_sem.at[1])
    own_slice.start()

    pl.semaphore_wait(barrier, 2 * (n - 1) + jnp.where(r != c, 1, 0))

    def current_copy(k, slot):
        return pltpu.make_async_remote_copy(
            src_ref=cur, dst_ref=cg.at[slot],
            send_sem=cg_send.at[k], recv_sem=cg_recv.at[k],
            device_id=(r, wrap(c + k)), device_id_type=MESH,
        )

    def slice_copy(k, slot):
        return pltpu.make_async_remote_copy(
            src_ref=at.at[:, wrap(c + k)], dst_ref=ra.at[slot],
            send_sem=ra_send.at[k], recv_sem=ra_recv.at[k],
            device_id=(r, wrap(c + k)), device_id_type=MESH,
        )

    def each(first, body):
        def step(k, carry):
            body(k)
            return carry

        lax.fori_loop(first, n, step, 0)

    each(1, lambda k: slice_copy(k, c).start())
    each(1, lambda k: current_copy(k, c).start())

    own_slice.wait()
    each(1, lambda k: slice_copy(k, wrap(c - k)).wait_recv())

    lane = lax.broadcasted_iota(jnp.int32, (16, 128), 1) // 16
    for i in range(12):
        block = slice((i // 8) * 128, (i // 8) * 128 + 128)
        for half in range(2):
            row = jnp.zeros((16, 128), F32)
            for t in range(8):
                x = ra[half * 8 + t, :, :, block].reshape(16, 128)
                shift = ((t - i % 8) * 16) % 128
                if shift:
                    x = pltpu.roll(x, shift, 1)
                row = jnp.where(lane == t, x, row)
            strip[3 + i, :, half * 128:half * 128 + 128] = row

    def edge_copy(d):
        src, dst, to = ((3, 15, wrap(r - 1)), (12, 0, wrap(r + 1)))[d]
        return pltpu.make_async_remote_copy(
            src_ref=strip.at[pl.ds(src, 3)], dst_ref=strip.at[pl.ds(dst, 3)],
            send_sem=halo_send.at[d], recv_sem=halo_recv.at[d],
            device_id=(to, c), device_id_type=MESH,
        )

    for d in range(2):
        edge_copy(d).start()

    column = lax.broadcasted_iota(jnp.int32, (16, 256), 1)

    def spread(e, carry):
        x = strip[e]
        for b in range(7):
            y = x if b == 3 else pltpu.roll(x, (3 - b) % 256, 1)
            if b < 3:
                y = jnp.where(column >= 3 - b, y, 0.0)
            if b > 3:
                y = jnp.where(column < 256 - (b - 3), y, 0.0)
            hi, lo = split(y)
            a7h[e, b * 16:b * 16 + 16, :] = hi
            a7l[e, b * 16:b * 16 + 16, :] = lo
        return carry

    lax.fori_loop(3, 15, spread, 0)

    own_current.wait()
    each(1, lambda k: current_copy(k, wrap(c - k)).wait_recv())

    def convert(t, carry):
        base = pl.multiple_of(t * 16, 16)
        for h in range(2):
            hi, lo = split(cg[t, :, pl.ds(h, 16, stride=2), :])
            chi[:, pl.ds(base, 16), h * 128:h * 128 + 128] = hi
            clo[:, pl.ds(base, 16), h * 128:h * 128 + 128] = lo
        return carry

    lax.fori_loop(0, n, convert, 0)

    acc[...] = jnp.zeros_like(acc)

    def correlate(i, carry):
        high = a7h[pl.ds(i, 7)].reshape(784, 256)
        low = a7l[pl.ds(i, 7)].reshape(784, 256)
        acc[...] += dot(high, chi[i]) + dot(low, chi[i]) + dot(high, clo[i])
        return carry

    lax.fori_loop(3, 9, correlate, 0)
    for d in range(2):
        edge_copy(d).wait_send()
        edge_copy(d).wait_recv()

    @pl.when(r == 0)
    def _():
        strip[0:3] = jnp.zeros((3, 16, 256), F32)

    @pl.when(r == n - 1)
    def _():
        strip[15:18] = jnp.zeros((3, 16, 256), F32)

    lax.fori_loop(0, 3, spread, 0)
    lax.fori_loop(15, 18, spread, 0)
    lax.fori_loop(0, 3, correlate, 0)
    lax.fori_loop(9, 12, correlate, 0)

    for a in range(7):
        x = acc[pl.ds(a * 112, 112), :].reshape(7, 2, 8, 256)
        real = x[:, 0, :, 0:128] + x[:, 1, :, 128:256]
        imag = x[:, 1, :, 0:128] - x[:, 0, :, 128:256]
        terms[a * 7:a * 7 + 7, 0] = real * factor
        terms[a * 7:a * 7 + 7, 1] = imag * factor
    terms[49:56] = jnp.zeros((7, 2, 8, 128), F32)

    def term_piece(p):
        return terms.at[pl.ds(0, 56)].reshape(112, 8, 128).at[pl.ds(p * 7, 7)]

    def reduce_copy(k, slot):
        return pltpu.make_async_remote_copy(
            src_ref=term_piece(wrap(r + k)), dst_ref=gathered.at[slot],
            send_sem=red_send.at[k], recv_sem=red_recv.at[k],
            device_id=(wrap(r + k), c), device_id_type=MESH,
        )

    each(1, lambda k: reduce_copy(k, r).start())
    own_piece = pltpu.make_async_copy(term_piece(r), gathered.at[r], own_sem.at[2])
    own_piece.start()
    own_piece.wait()
    each(1, lambda k: reduce_copy(k, wrap(r - k)).wait_recv())
    total = gathered[0]
    for k in range(1, n):
        total = total + gathered[k]
    piece[...] = total

    def swap_copy():
        return pltpu.make_async_remote_copy(
            src_ref=piece, dst_ref=swapped, send_sem=swap_send, recv_sem=swap_recv,
            device_id=(c, r), device_id_type=MESH,
        )

    @pl.when(r != c)
    def _():
        swap_copy().start()
        swap_copy().wait()

    @pl.when(r == c)
    def _():
        own = pltpu.make_async_copy(piece, swapped, own_sem.at[3])
        own.start()
        own.wait()

    def result_copy(k, slot):
        return pltpu.make_async_remote_copy(
            src_ref=swapped, dst_ref=result.at[pl.ds(slot * 7, 7)],
            send_sem=res_send.at[k], recv_sem=res_recv.at[k],
            device_id=(r, wrap(c + k)), device_id_type=MESH,
        )

    each(1, lambda k: result_copy(k, c).start())
    own_result = pltpu.make_async_copy(swapped, result.at[pl.ds(c * 7, 7)], own_sem.at[4])
    own_result.start()
    own_result.wait()
    each(1, lambda k: result_copy(k, wrap(c - k)).wait_recv())
    out[...] = result[0:98]

    def drain(k):
        slice_copy(k, c).wait_send()
        current_copy(k, c).wait_send()
        reduce_copy(k, r).wait_send()
        result_copy(k, c).wait_send()

    each(1, drain)


def params(collective_id):
    return pltpu.CompilerParams(
        collective_id=collective_id, has_side_effects=True, vmem_limit_bytes=60 * 1024 * 1024
    )


def on_device(adjoint_source, saved_currents, lag_blocks, element_inverse):
    vmem = pl.BlockSpec(memory_space=pltpu.VMEM)
    dma = pltpu.SemaphoreType.DMA
    tile = jax.ShapeDtypeStruct((12, 32, 128), F32)
    adjoint = pl.pallas_call(
        sweeps_kernel,
        out_shape=tile,
        in_specs=[vmem, pl.BlockSpec(memory_space=pl.ANY), vmem],
        out_specs=vmem,
        scratch_shapes=[
            pltpu.VMEM((7, 7, 2, 128, 128), F32),
            pltpu.VMEM((7, 1792, 256), BF16),
            pltpu.VMEM((7, 1792, 256), BF16),
            pltpu.VMEM((256, 256), BF16),
            pltpu.VMEM((256, 256), BF16),
            pltpu.VMEM((SWEEPS, 18, 48, 128), F32),
            pltpu.VMEM((18, 32, 1792), BF16),
            pltpu.VMEM((192, 256), F32),
            pltpu.VMEM((192, 256), F32),
            dma((7,)),
            dma((SWEEPS, 8)),
            dma((SWEEPS, 8)),
        ],
        compiler_params=params(0),
        name="sweeps",
    )(adjoint_source.reshape(12, 32, 128), lag_blocks, element_inverse)

    elements = 12 * lax.axis_size("row") * 16 * lax.axis_size("col")
    factor = -1.0 / math.sqrt(elements)
    lag_grad = pl.pallas_call(
        functools.partial(grads_kernel, factor),
        out_shape=jax.ShapeDtypeStruct((98, 8, 128), F32),
        in_specs=[vmem, vmem],
        out_specs=vmem,
        scratch_shapes=[
            pltpu.VMEM((16, 12, 32, 128), F32),
            pltpu.VMEM((12, 256, 256), BF16),
            pltpu.VMEM((12, 256, 256), BF16),
            pltpu.VMEM((2, 16, 8, 256), F32),
            pltpu.VMEM((16, 2, 8, 256), F32),
            pltpu.VMEM((18, 16, 256), F32),
            pltpu.VMEM((18, 112, 256), BF16),
            pltpu.VMEM((18, 112, 256), BF16),
            pltpu.VMEM((784, 256), F32),
            pltpu.VMEM((56, 2, 8, 128), F32),
            pltpu.VMEM((16, 7, 8, 128), F32),
            pltpu.VMEM((7, 8, 128), F32),
            pltpu.VMEM((7, 8, 128), F32),
            pltpu.VMEM((112, 8, 128), F32),
            dma((16,)), dma((16,)), dma((16,)), dma((16,)), dma((2,)), dma((2,)),
            dma((16,)), dma((16,)), dma(()), dma(()), dma((16,)), dma((16,)), dma((5,)),
        ],
        compiler_params=params(1),
        name="grads",
    )(adjoint, saved_currents.reshape(12, 32, 128))
    return (adjoint.reshape(12, 16, 2, 128), lag_grad.reshape(7, 7, 2, 8, 128))


def solution(mesh):
    return jax.shard_map(
        on_device,
        mesh=mesh,
        in_specs=(P("row", "col", None, None), P("row", "col", None, None), P(), P()),
        out_specs=(P("row", "col", None, None), P(None, None, None, "row", None)),
        check_vma=False,
    )
```

profile of v0, /device:TPU:1, one launch (start us, length us, event | category | flops | bytes accessed | tf_op | source)
XLA Modules:
  0.0 129.9 jit_solution(2156077422716068968)
XLA Ops:
  0.6 35.7 %sweeps.1.adj = f32[12,32,128]{2,1,0:T(8,128)} custom-call(f32[12,32,128]{2,1,0:T(8,128)} %bitcast.7, f32[7,7,2,128,128]{4,3,2,1,0:T(8,128)} %lag.1, f32[2,128,128]{2,1,0:T(8,128)} %inv.1), custom_call_target="tpu_custom_call" | custom-call | tf_op jit(solution)/shard_map/sweeps/pallas_call | solution.py:385
  36.3 90.1 %grads.1 = f32[98,8,128]{2,1,0:T(8,128)} custom-call(f32[12,32,128]{2,1,0:T(8,128)} %sweeps.1.adj, f32[12,32,128]{2,1,0:T(8,128)} %bitcast.6), custom_call_target="tpu_custom_call" | custom-call | tf_op jit(solution)/shard_map/grads/pallas_call | solution.py:410
  126.5 1.6 %copy.8 = f32[12,16,2,128]{3,2,1,0:T(2,128)} copy(f32[12,16,2,128]{3,2,1,0:T(2,128)} %bitcast.4) | data formatting | bytes 393216
  128.1 1.8 %copy.9 = f32[7,7,2,8,128]{4,3,2,1,0:T(8,128)} copy(f32[7,7,2,8,128]{4,3,2,1,0:T(8,128)} %bitcast.5) | data formatting | bytes 802816
where the time goes:
time: 130 us
  Pallas kernels  126 us (97%)
  local copies, waits for them, and re-layouts  3.39 us (3%)
    pallas_call x1, Pallas kernels, on_device(): pl.pallas_call(functools.partial(grads_kernel, factor), out_shape=jax.Sha...  90.1 us
    pallas_call x1, Pallas kernels, on_device(): pl.pallas_call(sweeps_kernel, out_shape=tile, in_specs=[vmem, pl.BlockSpe...  35.7 us
    unnamed x2, local copies, waits for them, and re-layouts  3.39 us

commit v1 on v0

v1 whole, which is shorter than its diff:
```python
import functools
import math

import jax
import jax.numpy as jnp
from jax import lax
from jax.experimental import pallas as pl
from jax.experimental.pallas import tpu as pltpu
from jax.sharding import PartitionSpec as P

SWEEPS = 2
F32 = jnp.float32
BF16 = jnp.bfloat16
MESH = pl.DeviceIdType.MESH
DIRS = tuple((dr, dc) for dr in (-1, 0, 1) for dc in (-1, 0, 1) if (dr, dc) != (0, 0))


def split(x):
    hi = x.astype(BF16)
    lo = (x - hi.astype(F32)).astype(BF16)
    return hi, lo


def dot(x, y):
    return jnp.dot(x, y, preferred_element_type=F32)


def put_embedded(dst, base, a0, a1):
    dst[pl.ds(base, 128), 0:128] = a0
    dst[pl.ds(base, 128), 128:256] = -a1
    dst[pl.ds(base + 128, 128), 0:128] = a1
    dst[pl.ds(base + 128, 128), 128:256] = a0


def field(ref, rows, start, cols):
    re = ref[rows, pl.ds(start, cols, stride=2), :]
    im = ref[rows, pl.ds(start + 1, cols, stride=2), :]
    return re, im

def kernel(
    factor, src, cur, lag, inv, out, grad,
    stage, whi, wlo, vhi, vlo, ext, shifted, total, adj,
    cg, chi, clo, at, ra, strip, a7h, a7l, terms, gathered, piece, swapped, result,
    lag_sem, send_sem, recv_sem, cg_send, cg_relay, cg_pass, cg_recv,
    ra_send, ra_recv, halo_send, halo_recv, red_send, red_recv,
    swap_send, swap_recv, res_send, res_recv, own_sem,
):
    n = 16
    r, c = lax.axis_index("row"), lax.axis_index("col")

    def wrap(x):
        return lax.rem(x + n, n)

    def lag_copy(a):
        return pltpu.make_async_copy(lag.at[a], stage.at[a], lag_sem.at[a])

    for a in range(7):
        lag_copy(a).start()
    own_current = pltpu.make_async_copy(cur, cg.at[c], own_sem.at[0])
    own_current.start()

    def each(first, body):
        def step(k, carry):
            body(k)
            return carry

        lax.fori_loop(first, n, step, 0)

    barrier = pltpu.get_barrier_semaphore()

    def greet(row, col):
        pl.semaphore_signal(barrier, inc=1, device_id=(row, col), device_id_type=MESH)

    each(1, lambda k: greet(r, wrap(c + k)))
    for dr in (-1, 1):
        for dc in (-1, 0, 1):
            greet(wrap(r + dr), wrap(c + dc))
    each(1, lambda k: greet(wrap(r + k), c))

    @pl.when(r != c)
    def _():
        greet(c, r)

    greetings = 15 + 6 + 15 + jnp.where(r != c, 1, 0)

    def box(dr, dc):
        rows = {-1: (3, 15, 3), 1: (12, 0, 3), 0: (3, 3, 12)}[dr]
        cols = {-1: (8, 40, 8), 1: (32, 0, 8), 0: (8, 8, 32)}[dc]
        return rows, cols

    def halo_copy(s, d):
        dr, dc = DIRS[d]
        (rs, rd, rn), (cs, cd, cn) = box(dr, dc)
        return pltpu.make_async_remote_copy(
            src_ref=ext.at[s, pl.ds(rs, rn), pl.ds(cs, cn), :],
            dst_ref=ext.at[s, pl.ds(rd, rn), pl.ds(cd, cn), :],
            send_sem=send_sem.at[s, d],
            recv_sem=recv_sem.at[s, d],
            device_id=(wrap(r + dr), wrap(c + dc)),
            device_id_type=MESH,
        )

    side, place, core = c // 8, lax.rem(c // 2, 4), lax.rem(c, 2)
    partner = c + 1 - 2 * core
    across = lax.rem(c + 8, n)

    def ring(dx):
        return side * 8 + lax.rem(place + dx, 4) * 2 + core

    def ring_across(dx):
        return lax.rem(ring(dx) + 8, n)

    def current_copy(slot, col, sem):
        return pltpu.make_async_remote_copy(
            src_ref=cg.at[slot], dst_ref=cg.at[slot],
            send_sem=sem, recv_sem=cg_recv.at[slot],
            device_id=(r, col), device_id_type=MESH,
        )

    def own_sends():
        return [current_copy(c, ring(dx), cg_send.at[dx]) for dx in (1, 3, 2)] + [
            current_copy(c, across, cg_send.at[0]),
            current_copy(c, partner, cg_send.at[4]),
        ]

    def relays():
        return [current_copy(across, ring(dx), cg_relay.at[dx]) for dx in (1, 3, 2)]

    def early_passes():
        slots = [ring(1), ring(3), ring(2), across]
        return [current_copy(x, partner, cg_pass.at[k]) for k, x in enumerate(slots)]

    def late_passes():
        slots = [ring_across(1), ring_across(3), ring_across(2)]
        return [current_copy(x, partner, cg_pass.at[4 + k]) for k, x in enumerate(slots)]

    b0h, b0l = split(inv[0])
    b1h, b1l = split(inv[1])
    put_embedded(vhi, 0, b0h, b1h)
    put_embedded(vlo, 0, b0l, b1l)

    def apply_inverse(x):
        xh, xl = split(x)
        return dot(xh, vhi[...]) + dot(xl, vhi[...]) + dot(xh, vlo[...])

    def source():
        re, im = field(src, slice(None), 0, 16)
        return jnp.concatenate([re.reshape(192, 128), im.reshape(192, 128)], axis=1)

    def publish(ref, at_, x):
        rows, start = at_
        ref[rows, pl.ds(start, 16, stride=2), :] = x[:, :128].reshape(12, 16, 128)
        ref[rows, pl.ds(start + 1, 16, stride=2), :] = x[:, 128:].reshape(12, 16, 128)

    adj[...] = apply_inverse(source())
    publish(ext.at[0], (slice(3, 15), 8), adj[...])
    own_current.wait()
    pl.semaphore_wait(barrier, greetings)

    for s in range(SWEEPS):
        for d in range(len(DIRS)):
            halo_copy(s, d).start()
        if s == 0:
            for copy in own_sends():
                copy.start()

            def prepare(a, carry):
                lag_copy(a).wait()

                def one(b, carry):
                    h0, l0 = split(stage[a, b, 0])
                    h1, l1 = split(stage[a, b, 1])
                    base = pl.multiple_of(b * 256, 256)
                    put_embedded(whi.at[a], base, h0, h1)
                    put_embedded(wlo.at[a], base, l0, l1)
                    return carry

                return lax.fori_loop(0, 7, one, carry)

            lax.fori_loop(0, 7, prepare, 0)
        else:
            for copy in early_passes():
                copy.wait_recv()
                copy.start()
            for copy in relays():
                copy.start()
        for d in range(len(DIRS)):
            halo_copy(s, d).wait_recv()

        @pl.when(r == 0)
        def _():
            ext[s, 0:3] = jnp.zeros((3, 48, 128), F32)

        @pl.when(r == n - 1)
        def _():
            ext[s, 15:18] = jnp.zeros((3, 48, 128), F32)

        @pl.when(c == 0)
        def _():
            ext[s, :, 0:8, :] = jnp.zeros((18, 8, 128), F32)

        @pl.when(c == n - 1)
        def _():
            ext[s, :, 40:48, :] = jnp.zeros((18, 8, 128), F32)

        for b in range(7):
            for h in range(2):
                hi, lo = split(ext[s, :, pl.ds(2 * (b + 1) + h, 16, stride=2), :])
                lanes = slice(b * 256 + h * 128, b * 256 + h * 128 + 128)
                shifted[:, 0:16, lanes] = hi
                shifted[:, 16:32, lanes] = lo

        total[...] = jnp.zeros_like(total)

        def lag_row(a, carry):
            both = dot(shifted[pl.ds(a, 12)].reshape(384, 1792), whi[a]).reshape(12, 32, 256)
            rest = dot(shifted[pl.ds(a, 12), 0:16, :].reshape(192, 1792), wlo[a])
            total[...] += (both[:, 0:16] + both[:, 16:32]).reshape(192, 256) + rest
            return carry

        lax.fori_loop(0, 7, lag_row, 0)
        adj[...] += apply_inverse(source() - adj[...] - total[...])
        if s + 1 < SWEEPS:
            publish(ext.at[s + 1], (slice(3, 15), 8), adj[...])

    for h in range(2):
        part = adj[:, h * 128:h * 128 + 128]
        part = jnp.concatenate([part, jnp.zeros((64, 128), F32)], axis=0)
        at[h] = part.T.reshape(16, 8, 256)

    def slice_copy(k, slot):
        return pltpu.make_async_remote_copy(
            src_ref=at.at[:, wrap(c + k)], dst_ref=ra.at[slot],
            send_sem=ra_send.at[k], recv_sem=ra_recv.at[k],
            device_id=(r, wrap(c + k)), device_id_type=MESH,
        )

    each(1, lambda k: slice_copy(k, c).start())
    own_slice = pltpu.make_async_copy(at.at[:, c], ra.at[c], own_sem.at[1])
    own_slice.start()
    publish(out, (slice(None), 0), adj[...])

    for copy in late_passes():
        copy.wait_recv()
        copy.start()

    def convert(t):
        base = pl.multiple_of(t * 16, 16)
        for h in range(2):
            hi, lo = split(cg[t, :, pl.ds(h, 16, stride=2), :])
            chi[:, pl.ds(base, 16), h * 128:h * 128 + 128] = hi
            clo[:, pl.ds(base, 16), h * 128:h * 128 + 128] = lo

    for dx in range(4):
        other = ring(dx) + 1 - 2 * core
        current_copy(other, partner, cg_send.at[4]).wait_recv()
        current_copy(lax.rem(other + 8, n), partner, cg_send.at[4]).wait_recv()
    lax.fori_loop(0, n, lambda t, carry: (convert(t), carry)[1], 0)

    own_slice.wait()
    each(1, lambda k: slice_copy(k, wrap(c - k)).wait_recv())

    lane = lax.broadcasted_iota(jnp.int32, (16, 128), 1) // 16
    for i in range(12):
        block = slice((i // 8) * 128, (i // 8) * 128 + 128)
        for half in range(2):
            row = jnp.zeros((16, 128), F32)
            for t in range(8):
                x = ra[half * 8 + t, :, :, block].reshape(16, 128)
                shift = ((t - i % 8) * 16) % 128
                if shift:
                    x = pltpu.roll(x, shift, 1)
                row = jnp.where(lane == t, x, row)
            strip[3 + i, :, half * 128:half * 128 + 128] = row

    def edge_copy(d):
        src_, dst, to = ((3, 15, wrap(r - 1)), (12, 0, wrap(r + 1)))[d]
        return pltpu.make_async_remote_copy(
            src_ref=strip.at[pl.ds(src_, 3)], dst_ref=strip.at[pl.ds(dst, 3)],
            send_sem=halo_send.at[d], recv_sem=halo_recv.at[d],
            device_id=(to, c), device_id_type=MESH,
        )

    for d in range(2):
        edge_copy(d).start()

    column = lax.broadcasted_iota(jnp.int32, (16, 256), 1)

    def spread(e, carry):
        x = strip[e]
        for b in range(7):
            y = x if b == 3 else pltpu.roll(x, (3 - b) % 256, 1)
            if b < 3:
                y = jnp.where(column >= 3 - b, y, 0.0)
            if b > 3:
                y = jnp.where(column < 256 - (b - 3), y, 0.0)
            hi, lo = split(y)
            a7h[e, b * 16:b * 16 + 16, :] = hi
            a7l[e, b * 16:b * 16 + 16, :] = lo
        return carry

    lax.fori_loop(3, 15, spread, 0)
    for d in range(2):
        edge_copy(d).wait_recv()

    @pl.when(r == 0)
    def _():
        strip[0:3] = jnp.zeros((3, 16, 256), F32)

    @pl.when(r == n - 1)
    def _():
        strip[15:18] = jnp.zeros((3, 16, 256), F32)

    lax.fori_loop(0, 3, spread, 0)
    lax.fori_loop(15, 18, spread, 0)

    def reduce_copy(p, slot):
        return pltpu.make_async_remote_copy(
            src_ref=terms.at[p], dst_ref=gathered.at[slot],
            send_sem=red_send.at[p], recv_sem=red_recv.at[slot],
            device_id=(p, c), device_id_type=MESH,
        )

    def keep_copy():
        return pltpu.make_async_copy(terms.at[r], gathered.at[r], own_sem.at[2])

    def correlate(a, carry):
        high = jnp.concatenate([a7h[a + i] for i in range(12)], axis=1)
        low = jnp.concatenate([a7l[a + i] for i in range(12)], axis=1)
        both = dot(jnp.concatenate([high, low], axis=0), chi[...].reshape(3072, 256))
        rest = dot(high, clo[...].reshape(3072, 256))
        x = (both[0:112] + both[112:224] + rest).reshape(7, 2, 8, 256)
        real = (x[:, 0, :, 0:128] + x[:, 1, :, 128:256]) * factor
        imag = (x[:, 1, :, 0:128] - x[:, 0, :, 128:256]) * factor
        for b in range(7):
            for h, part in ((0, real), (1, imag)):
                tile = b * 2 + h
                terms[a * 2 + tile // 7, tile % 7] = part[b]
        for e in range(2):
            p = a * 2 + e

            @pl.when(p != r)
            def _():
                reduce_copy(p, r).start()

            @pl.when(p == r)
            def _():
                keep_copy().start()

        return carry

    lax.fori_loop(0, 7, correlate, 0)

    @pl.when(r < 14)
    def _():
        def collect(k, carry):
            @pl.when(k == r)
            def _():
                keep_copy().wait()

            @pl.when(k != r)
            def _():
                reduce_copy(r, k).wait_recv()

            return carry

        lax.fori_loop(0, n, collect, 0)
        x = gathered[0]
        for k in range(1, n):
            x = x + gathered[k]
        piece[...] = x

    def swap_copy():
        return pltpu.make_async_remote_copy(
            src_ref=piece, dst_ref=swapped, send_sem=swap_send, recv_sem=swap_recv,
            device_id=(c, r), device_id_type=MESH,
        )

    @pl.when(jnp.logical_and(r != c, r < 14))
    def _():
        swap_copy().start()

    @pl.when(jnp.logical_and(r != c, c < 14))
    def _():
        swap_copy().wait_recv()

    @pl.when(jnp.logical_and(r == c, r < 14))
    def _():
        own = pltpu.make_async_copy(piece, swapped, own_sem.at[3])
        own.start()
        own.wait()

    @pl.when(jnp.logical_and(r != c, r < 14))
    def _():
        swap_copy().wait_send()

    def result_copy(k, slot):
        return pltpu.make_async_remote_copy(
            src_ref=swapped, dst_ref=result.at[slot],
            send_sem=res_send.at[k], recv_sem=res_recv.at[slot],
            device_id=(r, wrap(c + k)), device_id_type=MESH,
        )

    own_result = pltpu.make_async_copy(swapped, result.at[c], own_sem.at[4])

    @pl.when(c < 14)
    def _():
        each(1, lambda k: result_copy(k, c).start())
        own_result.start()

    def drain_reduce(p, carry):
        @pl.when(p != r)
        def _():
            reduce_copy(p, r).wait_send()

        return carry

    lax.fori_loop(0, 14, drain_reduce, 0)
    each(1, lambda k: slice_copy(k, c).wait_send())
    for copy in own_sends() + relays() + early_passes() + late_passes():
        copy.wait_send()
    for d in range(2):
        edge_copy(d).wait_send()
    for s in range(SWEEPS):
        for d in range(len(DIRS)):
            halo_copy(s, d).wait_send()

    def finish(p, carry):
        @pl.when(p == c)
        def _():
            own_result.wait()

        @pl.when(p != c)
        def _():
            result_copy(1, p).wait_recv()

        return carry

    lax.fori_loop(0, 14, finish, 0)
    grad[...] = result[0:14].reshape(98, 8, 128)

    @pl.when(c < 14)
    def _():
        each(1, lambda k: result_copy(k, c).wait_send())


def on_device(adjoint_source, saved_currents, lag_blocks, element_inverse):
    vmem = pl.BlockSpec(memory_space=pltpu.VMEM)
    hbm = pl.BlockSpec(memory_space=pl.ANY)
    dma = pltpu.SemaphoreType.DMA
    elements = 12 * lax.axis_size("row") * 16 * lax.axis_size("col")
    adjoint, lag_grad = pl.pallas_call(
        functools.partial(kernel, -1.0 / math.sqrt(elements)),
        out_shape=(
            jax.ShapeDtypeStruct((12, 32, 128), F32),
            jax.ShapeDtypeStruct((98, 8, 128), F32),
        ),
        in_specs=[vmem, hbm, hbm, vmem],
        out_specs=(vmem, vmem),
        scratch_shapes=[
            pltpu.VMEM((7, 7, 2, 128, 128), F32),
            pltpu.VMEM((7, 1792, 256), BF16),
            pltpu.VMEM((7, 1792, 256), BF16),
            pltpu.VMEM((256, 256), BF16),
            pltpu.VMEM((256, 256), BF16),
            pltpu.VMEM((SWEEPS, 18, 48, 128), F32),
            pltpu.VMEM((18, 32, 1792), BF16),
            pltpu.VMEM((192, 256), F32),
            pltpu.VMEM((192, 256), F32),
            pltpu.VMEM((16, 12, 32, 128), F32),
            pltpu.VMEM((12, 256, 256), BF16),
            pltpu.VMEM((12, 256, 256), BF16),
            pltpu.VMEM((2, 16, 8, 256), F32),
            pltpu.VMEM((16, 2, 8, 256), F32),
            pltpu.VMEM((18, 16, 256), F32),
            pltpu.VMEM((18, 112, 256), BF16),
            pltpu.VMEM((18, 112, 256), BF16),
            pltpu.VMEM((14, 7, 8, 128), F32),
            pltpu.VMEM((16, 7, 8, 128), F32),
            pltpu.VMEM((7, 8, 128), F32),
            pltpu.VMEM((7, 8, 128), F32),
            pltpu.VMEM((16, 7, 8, 128), F32),
            dma((7,)), dma((SWEEPS, 8)), dma((SWEEPS, 8)),
            dma((5,)), dma((4,)), dma((7,)), dma((16,)),
            dma((16,)), dma((16,)), dma((2,)), dma((2,)),
            dma((16,)), dma((16,)), dma(()), dma(()), dma((16,)), dma((16,)), dma((5,)),
        ],
        compiler_params=pltpu.CompilerParams(
            collective_id=0, has_side_effects=True, vmem_limit_bytes=62 * 1024 * 1024
        ),
        name="adjoint_gradient",
    )(
        adjoint_source.reshape(12, 32, 128),
        saved_currents.reshape(12, 32, 128),
        lag_blocks,
        element_inverse,
    )
    return (adjoint.reshape(12, 16, 2, 128), lag_grad.reshape(7, 7, 2, 8, 128))


def solution(mesh):
    return jax.shard_map(
        on_device,
        mesh=mesh,
        in_specs=(P("row", "col", None, None), P("row", "col", None, None), P(), P()),
        out_specs=(P("row", "col", None, None), P(None, None, None, "row", None)),
        check_vma=False,
    )
```

time: 130 us -> 84.9 us (0.65)
  Pallas kernels: 126 us -> 80.7 us
    pallas_call x2 -> x1, Pallas kernels: 126 us -> 80.7 us  [on_device(): pl.pallas_call(functools.partial(kernel, -1.0 / math.sqrt(elements)), out...]
where the time goes in v1:
time: 84.9 us; the launch traced here: 84.8 us
  Pallas kernels  80.7 us (95%)
  local copies, waits for them, and re-layouts  3.39 us (4%)
    pallas_call x1, Pallas kernels, on_device(): pl.pallas_call(functools.partial(kernel, -1.0 / math.sqrt(elements)), out...  80.7 us
    unnamed x2, local copies, waits for them, and re-layouts  3.39 us

profile of v1, /device:TPU:1, one launch (start us, length us, event | category | flops | bytes accessed | tf_op | source)
XLA Modules:
  0.0 84.8 jit_solution(17038947545475546848)
XLA Ops:
  0.6 80.7 %adjoint_gradient.1 = (f32[12,32,128]{2,1,0:T(8,128)}, f32[98,8,128]{2,1,0:T(8,128)}) custom-call(f32[12,32,128]{2,1,0:T(8,128)} %bitcast.6, f32[12,32,128]{2,1,0:T(8,128)} %bitcast.7, f32[7,7,2,128,128]{4,3,2,1,0:T(8,128)} %lag.1, f32[2,128,128]{2,1,0:T(8,128)} %inv.1), custom_call_target="tpu_custom_call" | custom-call | tf_op jit(solution)/shard_map/adjoint_gradient/pallas_call | solution.py:452
  81.4 1.6 %copy.8 = f32[12,16,2,128]{3,2,1,0:T(2,128)} copy(f32[12,16,2,128]{3,2,1,0:T(2,128)} %bitcast.5) | data formatting | bytes 393216
  83.0 1.8 %copy.9 = f32[7,7,2,8,128]{4,3,2,1,0:T(8,128)} copy(f32[7,7,2,8,128]{4,3,2,1,0:T(8,128)} %bitcast.4) | data formatting | bytes 802816

commit v2 on v1

--- a/solution.py
+++ b/solution.py
@@ -38,8 +38,8 @@
     return re, im
 
 def kernel(
-    factor, src, cur, lag, inv, out, grad,
-    stage, whi, wlo, vhi, vlo, ext, shifted, total, adj,
+    factor, src_hbm, cur, lag, inv_hbm, out, grad,
+    src, inv, stage, whi, wlo, vhi, vlo, ext, near_hi, near_lo, total, adj,
     cg, chi, clo, at, ra, strip, a7h, a7l, terms, gathered, piece, swapped, result,
     lag_sem, send_sem, recv_sem, cg_send, cg_relay, cg_pass, cg_recv,
     ra_send, ra_recv, halo_send, halo_recv, red_send, red_recv,
@@ -51,6 +51,11 @@
     def wrap(x):
         return lax.rem(x + n, n)
 
+    src_copy = pltpu.make_async_copy(src_hbm, src, own_sem.at[5])
+    inv_copy = pltpu.make_async_copy(inv_hbm, inv, own_sem.at[6])
+    src_copy.start()
+    inv_copy.start()
+
     def lag_copy(a):
         return pltpu.make_async_copy(lag.at[a], stage.at[a], lag_sem.at[a])
 
@@ -134,6 +139,8 @@
         slots = [ring_across(1), ring_across(3), ring_across(2)]
         return [current_copy(x, partner, cg_pass.at[4 + k]) for k, x in enumerate(slots)]
 
+    inv_copy.wait()
+    src_copy.wait()
     b0h, b0l = split(inv[0])
     b1h, b1l = split(inv[1])
     put_embedded(vhi, 0, b0h, b1h)
@@ -157,10 +164,11 @@
     own_current.wait()
     pl.semaphore_wait(barrier, greetings)
 
-    for s in range(SWEEPS):
+    def sweep(s, carry):
         for d in range(len(DIRS)):
             halo_copy(s, d).start()
-        if s == 0:
+        @pl.when(s == 0)
+        def _():
             for copy in own_sends():
                 copy.start()
 
@@ -178,12 +186,15 @@
                 return lax.fori_loop(0, 7, one, carry)
 
             lax.fori_loop(0, 7, prepare, 0)
-        else:
+
+        @pl.when(s > 0)
+        def _():
             for copy in early_passes():
                 copy.wait_recv()
                 copy.start()
             for copy in relays():
                 copy.start()
+
         for d in range(len(DIRS)):
             halo_copy(s, d).wait_recv()
 
@@ -207,21 +218,26 @@
             for h in range(2):
                 hi, lo = split(ext[s, :, pl.ds(2 * (b + 1) + h, 16, stride=2), :])
                 lanes = slice(b * 256 + h * 128, b * 256 + h * 128 + 128)
-                shifted[:, 0:16, lanes] = hi
-                shifted[:, 16:32, lanes] = lo
+                near_hi[:, :, lanes] = hi
+                near_lo[:, :, lanes] = lo
 
         total[...] = jnp.zeros_like(total)
 
         def lag_row(a, carry):
-            both = dot(shifted[pl.ds(a, 12)].reshape(384, 1792), whi[a]).reshape(12, 32, 256)
-            rest = dot(shifted[pl.ds(a, 12), 0:16, :].reshape(192, 1792), wlo[a])
-            total[...] += (both[:, 0:16] + both[:, 16:32]).reshape(192, 256) + rest
+            hi = near_hi[pl.ds(a, 12)].reshape(192, 1792)
+            lo = near_lo[pl.ds(a, 12)].reshape(192, 1792)
+            total[...] += dot(hi, whi[a]) + dot(lo, whi[a]) + dot(hi, wlo[a])
             return carry
 
         lax.fori_loop(0, 7, lag_row, 0)
         adj[...] += apply_inverse(source() - adj[...] - total[...])
-        if s + 1 < SWEEPS:
-            publish(ext.at[s + 1], (slice(3, 15), 8), adj[...])
+        @pl.when(s + 1 < SWEEPS)
+        def _():
+            publish(ext.at[lax.rem(s + 1, SWEEPS)], (slice(3, 15), 8), adj[...])
+
+        return carry
+
+    lax.fori_loop(0, SWEEPS, sweep, 0)
 
     for h in range(2):
         part = adj[:, h * 128:h * 128 + 128]
@@ -444,6 +460,24 @@
         each(1, lambda k: result_copy(k, c).wait_send())
 
 
+def hand_out(adj, grad, adj_out, grad_out, adj_buf, grad_buf, sem):
+    into = [
+        pltpu.make_async_copy(adj, adj_buf, sem.at[0]),
+        pltpu.make_async_copy(grad, grad_buf, sem.at[1]),
+    ]
+    back = [
+        pltpu.make_async_copy(adj_buf, adj_out, sem.at[2]),
+        pltpu.make_async_copy(grad_buf, grad_out, sem.at[3]),
+    ]
+    for copy in into:
+        copy.start()
+    for first, second in zip(into, back):
+        first.wait()
+        second.start()
+    for copy in back:
+        copy.wait()
+
+
 def on_device(adjoint_source, saved_currents, lag_blocks, element_inverse):
     vmem = pl.BlockSpec(memory_space=pltpu.VMEM)
     hbm = pl.BlockSpec(memory_space=pl.ANY)
@@ -455,16 +489,19 @@
             jax.ShapeDtypeStruct((12, 32, 128), F32),
             jax.ShapeDtypeStruct((98, 8, 128), F32),
         ),
-        in_specs=[vmem, hbm, hbm, vmem],
+        in_specs=[pl.BlockSpec(memory_space=pltpu.HBM)] * 4,
         out_specs=(vmem, vmem),
         scratch_shapes=[
+            pltpu.VMEM((12, 32, 128), F32),
+            pltpu.VMEM((2, 128, 128), F32),
             pltpu.VMEM((7, 7, 2, 128, 128), F32),
             pltpu.VMEM((7, 1792, 256), BF16),
             pltpu.VMEM((7, 1792, 256), BF16),
             pltpu.VMEM((256, 256), BF16),
             pltpu.VMEM((256, 256), BF16),
             pltpu.VMEM((SWEEPS, 18, 48, 128), F32),
-            pltpu.VMEM((18, 32, 1792), BF16),
+            pltpu.VMEM((18, 16, 1792), BF16),
+            pltpu.VMEM((18, 16, 1792), BF16),
             pltpu.VMEM((192, 256), F32),
             pltpu.VMEM((192, 256), F32),
             pltpu.VMEM((16, 12, 32, 128), F32),
@@ -483,7 +520,7 @@
             dma((7,)), dma((SWEEPS, 8)), dma((SWEEPS, 8)),
             dma((5,)), dma((4,)), dma((7,)), dma((16,)),
             dma((16,)), dma((16,)), dma((2,)), dma((2,)),
-            dma((16,)), dma((16,)), dma(()), dma(()), dma((16,)), dma((16,)), dma((5,)),
+            dma((16,)), dma((16,)), dma(()), dma(()), dma((16,)), dma((16,)), dma((7,)),
         ],
         compiler_params=pltpu.CompilerParams(
             collective_id=0, has_side_effects=True, vmem_limit_bytes=62 * 1024 * 1024
@@ -495,6 +532,20 @@
         lag_blocks,
         element_inverse,
     )
+    adjoint, lag_grad = pl.pallas_call(
+        hand_out,
+        out_shape=(
+            jax.ShapeDtypeStruct((12, 32, 128), F32),
+            jax.ShapeDtypeStruct((98, 8, 128), F32),
+        ),
+        in_specs=[hbm, hbm],
+        out_specs=(hbm, hbm),
+        scratch_shapes=[
+            pltpu.VMEM((12, 32, 128), F32), pltpu.VMEM((98, 8, 128), F32), dma((4,)),
+        ],
+        compiler_params=pltpu.CompilerParams(vmem_limit_bytes=62 * 1024 * 1024),
+        name="hand_out",
+    )(adjoint, lag_grad)
     return (adjoint.reshape(12, 16, 2, 128), lag_grad.reshape(7, 7, 2, 8, 128))
 
 

time: 84.9 us -> 80.2 us (0.945)
  local copies, waits for them, and re-layouts: 3.39 us -> 0 us
  Pallas kernels: 80.7 us -> 79.5 us
    unnamed x2 -> x0, local copies, waits for them, and re-layouts: 3.39 us -> none
    pallas_call x1, Pallas kernels: 80.7 us -> 77.6 us  [on_device(): pl.pallas_call(functools.partial(kernel, -1.0 / math.sqrt(elements)), out...]
    pallas_call x0 -> x1, Pallas kernels: none -> 1.89 us  [on_device(): pl.pallas_call(hand_out, out_shape=(jax.ShapeDtypeStruct((12, 32, 128), F...]
where the time goes in v2:
time: 80.2 us; the launch traced here: 80.1 us
  Pallas kernels  79.5 us (99%)
    pallas_call x1, Pallas kernels, on_device(): pl.pallas_call(functools.partial(kernel, -1.0 / math.sqrt(elements)), out...  77.6 us
    pallas_call x1, Pallas kernels, on_device(): pl.pallas_call(hand_out, out_shape=(jax.ShapeDtypeStruct((12, 32, 128), F...  1.89 us

profile of v2, /device:TPU:1, one launch (start us, length us, event | category | flops | bytes accessed | tf_op | source)
XLA Modules:
  0.0 80.1 jit_solution(15447275422206353658)
XLA Ops:
  0.6 77.6 %adjoint_gradient.1 = (f32[12,32,128]{2,1,0:T(8,128)}, f32[98,8,128]{2,1,0:T(8,128)}) custom-call(f32[12,32,128]{2,1,0:T(8,128)} %bitcast.4, f32[12,32,128]{2,1,0:T(8,128)} %bitcast.5, f32[7,7,2,128,128]{4,3,2,1,0:T(8,128)} %lag.1, f32[2,128,128]{2,1,0:T(8,128)} %inv_hbm.1), custom_call_target="tpu_custom_call" | custom-call | tf_op jit(solution)/shard_map/adjoint_gradient/pallas_call | solution.py:486
  78.2 1.9 %hand_out.1 = (f32[12,32,128]{2,1,0:T(8,128)}, f32[98,8,128]{2,1,0:T(8,128)}) custom-call(f32[12,32,128]{2,1,0:T(8,128)} %get-tuple-element.6.adj, f32[98,8,128]{2,1,0:T(8,128)} %get-tuple-element.7.grad), custom_call_target="tpu_custom_call" | custom-call | tf_op jit(solution)/shard_map/hand_out/pallas_call | solution.py:535

commit v3 on v2

--- a/solution.py
+++ b/solution.py
@@ -12,7 +12,9 @@
 F32 = jnp.float32
 BF16 = jnp.bfloat16
 MESH = pl.DeviceIdType.MESH
-DIRS = tuple((dr, dc) for dr in (-1, 0, 1) for dc in (-1, 0, 1) if (dr, dc) != (0, 0))
+DIRS = ((-1, -1), (-1, 1), (1, -1), (1, 1), (0, -1), (0, 1), (-1, 0), (1, 0))
+SIDES = (4, 5)
+REST = (0, 1, 2, 3, 6, 7)
 
 
 def split(x):
@@ -164,6 +166,9 @@
     own_current.wait()
     pl.semaphore_wait(barrier, greetings)
 
+    def middle_first(t):
+        return jnp.where(t == 0, 3, jnp.where(t < 4, t - 1, t))
+
     def sweep(s, carry):
         for d in range(len(DIRS)):
             halo_copy(s, d).start()
@@ -195,35 +200,50 @@
             for copy in relays():
                 copy.start()
 
-        for d in range(len(DIRS)):
+        def close_sides(rows, count):
+            @pl.when(c == 0)
+            def _():
+                ext[s, rows, 0:8, :] = jnp.zeros((count, 8, 128), F32)
+
+            @pl.when(c == n - 1)
+            def _():
+                ext[s, rows, 40:48, :] = jnp.zeros((count, 8, 128), F32)
+
+        def build(rows):
+            for b in range(7):
+                for h in range(2):
+                    hi, lo = split(ext[s, rows, pl.ds(2 * (b + 1) + h, 16, stride=2), :])
+                    lanes = slice(b * 256 + h * 128, b * 256 + h * 128 + 128)
+                    near_hi[rows, :, lanes] = hi
+                    near_lo[rows, :, lanes] = lo
+
+        for d in SIDES:
             halo_copy(s, d).wait_recv()
-
-        @pl.when(r == 0)
-        def _():
-            ext[s, 0:3] = jnp.zeros((3, 48, 128), F32)
-
-        @pl.when(r == n - 1)
-        def _():
-            ext[s, 15:18] = jnp.zeros((3, 48, 128), F32)
-
-        @pl.when(c == 0)
-        def _():
-            ext[s, :, 0:8, :] = jnp.zeros((18, 8, 128), F32)
-
-        @pl.when(c == n - 1)
-        def _():
-            ext[s, :, 40:48, :] = jnp.zeros((18, 8, 128), F32)
-
-        for b in range(7):
-            for h in range(2):
-                hi, lo = split(ext[s, :, pl.ds(2 * (b + 1) + h, 16, stride=2), :])
-                lanes = slice(b * 256 + h * 128, b * 256 + h * 128 + 128)
-                near_hi[:, :, lanes] = hi
-                near_lo[:, :, lanes] = lo
-
+        close_sides(slice(3, 15), 12)
+        build(slice(3, 15))
         total[...] = jnp.zeros_like(total)
 
-        def lag_row(a, carry):
+        def lag_row(t, carry):
+            a = middle_first(t)
+
+            @pl.when(t == 1)
+            def _():
+                for d in REST:
+                    halo_copy(s, d).wait_recv()
+
+                @pl.when(r == 0)
+                def _():
+                    ext[s, 0:3] = jnp.zeros((3, 48, 128), F32)
+
+                @pl.when(r == n - 1)
+                def _():
+                    ext[s, 15:18] = jnp.zeros((3, 48, 128), F32)
+
+                close_sides(slice(0, 3), 3)
+                close_sides(slice(15, 18), 3)
+                build(slice(0, 3))
+                build(slice(15, 18))
+
             hi = near_hi[pl.ds(a, 12)].reshape(192, 1792)
             lo = near_lo[pl.ds(a, 12)].reshape(192, 1792)
             total[...] += dot(hi, whi[a]) + dot(lo, whi[a]) + dot(hi, wlo[a])
@@ -316,19 +336,6 @@
         return carry
 
     lax.fori_loop(3, 15, spread, 0)
-    for d in range(2):
-        edge_copy(d).wait_recv()
-
-    @pl.when(r == 0)
-    def _():
-        strip[0:3] = jnp.zeros((3, 16, 256), F32)
-
-    @pl.when(r == n - 1)
-    def _():
-        strip[15:18] = jnp.zeros((3, 16, 256), F32)
-
-    lax.fori_loop(0, 3, spread, 0)
-    lax.fori_loop(15, 18, spread, 0)
 
     def reduce_copy(p, slot):
         return pltpu.make_async_remote_copy(
@@ -340,7 +347,25 @@
     def keep_copy():
         return pltpu.make_async_copy(terms.at[r], gathered.at[r], own_sem.at[2])
 
-    def correlate(a, carry):
+    def correlate(t, carry):
+        a = middle_first(t)
+
+        @pl.when(t == 1)
+        def _():
+            for d in range(2):
+                edge_copy(d).wait_recv()
+
+            @pl.when(r == 0)
+            def _():
+                strip[0:3] = jnp.zeros((3, 16, 256), F32)
+
+            @pl.when(r == n - 1)
+            def _():
+                strip[15:18] = jnp.zeros((3, 16, 256), F32)
+
+            lax.fori_loop(0, 3, spread, 0)
+            lax.fori_loop(15, 18, spread, 0)
+
         high = jnp.concatenate([a7h[a + i] for i in range(12)], axis=1)
         low = jnp.concatenate([a7l[a + i] for i in range(12)], axis=1)
         both = dot(jnp.concatenate([high, low], axis=0), chi[...].reshape(3072, 256))

time: 80.2 us -> 77.8 us (0.970)
  Pallas kernels: 79.5 us -> 77.1 us
    pallas_call x1, Pallas kernels: 77.6 us -> 75.2 us  [on_device(): pl.pallas_call(functools.partial(kernel, -1.0 / math.sqrt(elements)), out...]
where the time goes in v3:
time: 77.8 us; the launch traced here: 77.7 us
  Pallas kernels  77.1 us (99%)
    pallas_call x1, Pallas kernels, on_device(): pl.pallas_call(functools.partial(kernel, -1.0 / math.sqrt(elements)), out...  75.2 us
    pallas_call x1, Pallas kernels, on_device(): pl.pallas_call(hand_out, out_shape=(jax.ShapeDtypeStruct((12, 32, 128), F...  1.89 us

profile of v3, /device:TPU:1, one launch (start us, length us, event | category | flops | bytes accessed | tf_op | source)
XLA Modules:
  0.0 77.7 jit_solution(1544378850255988779)
XLA Ops:
  0.6 75.2 %adjoint_gradient.1 = (f32[12,32,128]{2,1,0:T(8,128)}, f32[98,8,128]{2,1,0:T(8,128)}) custom-call(f32[12,32,128]{2,1,0:T(8,128)} %bitcast.4, f32[12,32,128]{2,1,0:T(8,128)} %bitcast.5, f32[7,7,2,128,128]{4,3,2,1,0:T(8,128)} %lag.1, f32[2,128,128]{2,1,0:T(8,128)} %inv_hbm.1), custom_call_target="tpu_custom_call" | custom-call | tf_op jit(solution)/shard_map/adjoint_gradient/pallas_call | solution.py:511
  75.8 1.9 %hand_out.1 = (f32[12,32,128]{2,1,0:T(8,128)}, f32[98,8,128]{2,1,0:T(8,128)}) custom-call(f32[12,32,128]{2,1,0:T(8,128)} %get-tuple-element.6.adj, f32[98,8,128]{2,1,0:T(8,128)} %get-tuple-element.7.grad), custom_call_target="tpu_custom_call" | custom-call | tf_op jit(solution)/shard_map/hand_out/pallas_call | solution.py:560

commit v4 on v3

--- a/solution.py
+++ b/solution.py
@@ -41,30 +41,17 @@
 
 def kernel(
     factor, src_hbm, cur, lag, inv_hbm, out, grad,
-    src, inv, stage, whi, wlo, vhi, vlo, ext, near_hi, near_lo, total, adj,
+    src, inv, out_tile, stage, whi, wlo, vhi, vlo, ext, near_hi, near_lo, total, adj,
     cg, chi, clo, at, ra, strip, a7h, a7l, terms, gathered, piece, swapped, result,
     lag_sem, send_sem, recv_sem, cg_send, cg_relay, cg_pass, cg_recv,
     ra_send, ra_recv, halo_send, halo_recv, red_send, red_recv,
-    swap_send, swap_recv, res_send, res_recv, own_sem,
+    swap_send, swap_recv, res_send, res_recv, own_sem, out_sem,
 ):
     n = 16
     r, c = lax.axis_index("row"), lax.axis_index("col")
 
     def wrap(x):
         return lax.rem(x + n, n)
-
-    src_copy = pltpu.make_async_copy(src_hbm, src, own_sem.at[5])
-    inv_copy = pltpu.make_async_copy(inv_hbm, inv, own_sem.at[6])
-    src_copy.start()
-    inv_copy.start()
-
-    def lag_copy(a):
-        return pltpu.make_async_copy(lag.at[a], stage.at[a], lag_sem.at[a])
-
-    for a in range(7):
-        lag_copy(a).start()
-    own_current = pltpu.make_async_copy(cur, cg.at[c], own_sem.at[0])
-    own_current.start()
 
     def each(first, body):
         def step(k, carry):
@@ -84,11 +71,20 @@
             greet(wrap(r + dr), wrap(c + dc))
     each(1, lambda k: greet(wrap(r + k), c))
 
-    @pl.when(r != c)
-    def _():
-        greet(c, r)
-
-    greetings = 15 + 6 + 15 + jnp.where(r != c, 1, 0)
+    greetings = 15 + 6 + 15
+
+    src_copy = pltpu.make_async_copy(src_hbm, src, own_sem.at[5])
+    inv_copy = pltpu.make_async_copy(inv_hbm, inv, own_sem.at[6])
+    src_copy.start()
+    inv_copy.start()
+
+    def lag_copy(a):
+        return pltpu.make_async_copy(lag.at[a], stage.at[a], lag_sem.at[a])
+
+    for a in range(7):
+        lag_copy(a).start()
+    own_current = pltpu.make_async_copy(cur, cg.at[c], own_sem.at[0])
+    own_current.start()
 
     def box(dr, dc):
         rows = {-1: (3, 15, 3), 1: (12, 0, 3), 0: (3, 3, 12)}[dr]
@@ -274,7 +270,9 @@
     each(1, lambda k: slice_copy(k, c).start())
     own_slice = pltpu.make_async_copy(at.at[:, c], ra.at[c], own_sem.at[1])
     own_slice.start()
-    publish(out, (slice(None), 0), adj[...])
+    publish(out_tile, (slice(None), 0), adj[...])
+    out_copy = pltpu.make_async_copy(out_tile, out, out_sem.at[14])
+    out_copy.start()
 
     for copy in late_passes():
         copy.wait_recv()
@@ -466,6 +464,9 @@
         for d in range(len(DIRS)):
             halo_copy(s, d).wait_send()
 
+    def grad_copy(p):
+        return pltpu.make_async_copy(result.at[p], grad.at[pl.ds(p * 7, 7)], out_sem.at[p])
+
     def finish(p, carry):
         @pl.when(p == c)
         def _():
@@ -475,10 +476,12 @@
         def _():
             result_copy(1, p).wait_recv()
 
+        grad_copy(p).start()
         return carry
 
     lax.fori_loop(0, 14, finish, 0)
-    grad[...] = result[0:14].reshape(98, 8, 128)
+    out_copy.wait()
+    lax.fori_loop(0, 14, lambda p, carry: (grad_copy(p).wait(), carry)[1], 0)
 
     @pl.when(c < 14)
     def _():
@@ -504,7 +507,6 @@
 
 
 def on_device(adjoint_source, saved_currents, lag_blocks, element_inverse):
-    vmem = pl.BlockSpec(memory_space=pltpu.VMEM)
     hbm = pl.BlockSpec(memory_space=pl.ANY)
     dma = pltpu.SemaphoreType.DMA
     elements = 12 * lax.axis_size("row") * 16 * lax.axis_size("col")
@@ -515,10 +517,11 @@
             jax.ShapeDtypeStruct((98, 8, 128), F32),
         ),
         in_specs=[pl.BlockSpec(memory_space=pltpu.HBM)] * 4,
-        out_specs=(vmem, vmem),
+        out_specs=(pl.BlockSpec(memory_space=pltpu.HBM),) * 2,
         scratch_shapes=[
             pltpu.VMEM((12, 32, 128), F32),
             pltpu.VMEM((2, 128, 128), F32),
+            pltpu.VMEM((12, 32, 128), F32),
             pltpu.VMEM((7, 7, 2, 128, 128), F32),
             pltpu.VMEM((7, 1792, 256), BF16),
             pltpu.VMEM((7, 1792, 256), BF16),
@@ -545,7 +548,7 @@
             dma((7,)), dma((SWEEPS, 8)), dma((SWEEPS, 8)),
             dma((5,)), dma((4,)), dma((7,)), dma((16,)),
             dma((16,)), dma((16,)), dma((2,)), dma((2,)),
-            dma((16,)), dma((16,)), dma(()), dma(()), dma((16,)), dma((16,)), dma((7,)),
+            dma((16,)), dma((16,)), dma(()), dma(()), dma((16,)), dma((16,)), dma((7,)), dma((15,)),
         ],
         compiler_params=pltpu.CompilerParams(
             collective_id=0, has_side_effects=True, vmem_limit_bytes=62 * 1024 * 1024

time: 77.8 us -> 77.4 us (level)
  no operation moved by 1% of the time
where the time goes in v4:
time: 77.4 us; the launch traced here: 77.3 us
  Pallas kernels  76.6 us (99%)
    pallas_call x1, Pallas kernels, on_device(): pl.pallas_call(functools.partial(kernel, -1.0 / math.sqrt(elements)), out...  74.7 us
    pallas_call x1, Pallas kernels, on_device(): pl.pallas_call(hand_out, out_shape=(jax.ShapeDtypeStruct((12, 32, 128), F...  1.89 us

profile of v4, /device:TPU:1, one launch (start us, length us, event | category | flops | bytes accessed | tf_op | source)
XLA Modules:
  0.0 77.3 jit_solution(8222535775446632124)
XLA Ops:
  0.6 74.7 %adjoint_gradient.1 = (f32[12,32,128]{2,1,0:T(8,128)}, f32[98,8,128]{2,1,0:T(8,128)}) custom-call(f32[12,32,128]{2,1,0:T(8,128)} %bitcast.4, f32[12,32,128]{2,1,0:T(8,128)} %bitcast.5, f32[7,7,2,128,128]{4,3,2,1,0:T(8,128)} %lag.1, f32[2,128,128]{2,1,0:T(8,128)} %inv_hbm.1), custom_call_target="tpu_custom_call" | custom-call | tf_op jit(solution)/shard_map/adjoint_gradient/pallas_call | solution.py:513
  75.4 1.9 %hand_out.1 = (f32[12,32,128]{2,1,0:T(8,128)}, f32[98,8,128]{2,1,0:T(8,128)}) custom-call(f32[12,32,128]{2,1,0:T(8,128)} %get-tuple-element.6.adj, f32[98,8,128]{2,1,0:T(8,128)} %get-tuple-element.7.grad), custom_call_target="tpu_custom_call" | custom-call | tf_op jit(solution)/shard_map/hand_out/pallas_call | solution.py:563

commit v5 on v4

--- a/solution.py
+++ b/solution.py
@@ -346,7 +346,8 @@
         return pltpu.make_async_copy(terms.at[r], gathered.at[r], own_sem.at[2])
 
     def correlate(t, carry):
-        a = middle_first(t)
+        other = lax.rem(r // 2 + t, 6)
+        a = jnp.where(t == 0, 3, other + jnp.where(other >= 3, 1, 0))
 
         @pl.when(t == 1)
         def _():

time: 77.4 us -> 74.2 us (0.959)
  Pallas kernels: 76.6 us -> 73.5 us
    pallas_call x1, Pallas kernels: 74.7 us -> 71.6 us  [on_device(): pl.pallas_call(functools.partial(kernel, -1.0 / math.sqrt(elements)), out...]
where the time goes in v5:
time: 74.2 us; the launch traced here: 74.1 us
  Pallas kernels  73.5 us (99%)
    pallas_call x1, Pallas kernels, on_device(): pl.pallas_call(functools.partial(kernel, -1.0 / math.sqrt(elements)), out...  71.6 us
    pallas_call x1, Pallas kernels, on_device(): pl.pallas_call(hand_out, out_shape=(jax.ShapeDtypeStruct((12, 32, 128), F...  1.89 us

profile of v5, /device:TPU:1, one launch (start us, length us, event | category | flops | bytes accessed | tf_op | source)
XLA Modules:
  0.0 74.1 jit_solution(7436024072189678449)
XLA Ops:
  0.6 71.6 %adjoint_gradient.1 = (f32[12,32,128]{2,1,0:T(8,128)}, f32[98,8,128]{2,1,0:T(8,128)}) custom-call(f32[12,32,128]{2,1,0:T(8,128)} %bitcast.4, f32[12,32,128]{2,1,0:T(8,128)} %bitcast.5, f32[7,7,2,128,128]{4,3,2,1,0:T(8,128)} %lag.1, f32[2,128,128]{2,1,0:T(8,128)} %inv_hbm.1), custom_call_target="tpu_custom_call" | custom-call | tf_op jit(solution)/shard_map/adjoint_gradient/pallas_call | solution.py:514
  72.2 1.9 %hand_out.1 = (f32[12,32,128]{2,1,0:T(8,128)}, f32[98,8,128]{2,1,0:T(8,128)}) custom-call(f32[12,32,128]{2,1,0:T(8,128)} %get-tuple-element.6.adj, f32[98,8,128]{2,1,0:T(8,128)} %get-tuple-element.7.grad), custom_call_target="tpu_custom_call" | custom-call | tf_op jit(solution)/shard_map/hand_out/pallas_call | solution.py:564

commit v6 on v5

--- a/solution.py
+++ b/solution.py
@@ -346,7 +346,7 @@
         return pltpu.make_async_copy(terms.at[r], gathered.at[r], own_sem.at[2])
 
     def correlate(t, carry):
-        other = lax.rem(r // 2 + t, 6)
+        other = lax.rem(r // 2 + jnp.where(core == 0, t, 6 - t), 6)
         a = jnp.where(t == 0, 3, other + jnp.where(other >= 3, 1, 0))
 
         @pl.when(t == 1)

time: 74.2 us -> 74.9 us (level)
  no operation moved by 1% of the time
where the time goes in v6:
time: 74.9 us; the launch traced here: 74.8 us
  Pallas kernels  74.1 us (99%)
    pallas_call x1, Pallas kernels, on_device(): pl.pallas_call(functools.partial(kernel, -1.0 / math.sqrt(elements)), out...  72.2 us
    pallas_call x1, Pallas kernels, on_device(): pl.pallas_call(hand_out, out_shape=(jax.ShapeDtypeStruct((12, 32, 128), F...  1.89 us

profile of v6, /device:TPU:1, one launch (start us, length us, event | category | flops | bytes accessed | tf_op | source)
XLA Modules:
  0.0 74.8 jit_solution(6606281613765470566)
XLA Ops:
  0.6 72.2 %adjoint_gradient.1 = (f32[12,32,128]{2,1,0:T(8,128)}, f32[98,8,128]{2,1,0:T(8,128)}) custom-call(f32[12,32,128]{2,1,0:T(8,128)} %bitcast.4, f32[12,32,128]{2,1,0:T(8,128)} %bitcast.5, f32[7,7,2,128,128]{4,3,2,1,0:T(8,128)} %lag.1, f32[2,128,128]{2,1,0:T(8,128)} %inv_hbm.1), custom_call_target="tpu_custom_call" | custom-call | tf_op jit(solution)/shard_map/adjoint_gradient/pallas_call | solution.py:514
  72.9 1.9 %hand_out.1 = (f32[12,32,128]{2,1,0:T(8,128)}, f32[98,8,128]{2,1,0:T(8,128)}) custom-call(f32[12,32,128]{2,1,0:T(8,128)} %get-tuple-element.6.adj, f32[98,8,128]{2,1,0:T(8,128)} %get-tuple-element.7.grad), custom_call_target="tpu_custom_call" | custom-call | tf_op jit(solution)/shard_map/hand_out/pallas_call | solution.py:564
